TPU v7x, 256 devices: a whole 4x4x8 slice. The times are simulated.
256 devices in a mesh: expert: 32 (over z, y), etp: 8 (over x, core).
Axes of the slice: x: 4, y: 4, z: 8, core: 2. Of those that a mesh axis runs over, the one named last changes fastest.
Arguments:
- tokens: bfloat16 [32768, 2560], P(('expert', 'etp')), may hold values from -6 to 6
- grad_out: bfloat16 [32768, 2560], P(('expert', 'etp')), may hold values from -6 to 6
- router_weight: bfloat16 [2560, 32], replicated, may hold values from -0.125 to 0.125
- expert_choice: int32 [32768, 1], P(('expert', 'etp')), may hold values from 0 to 31; in each aligned block of 128 rows (0 to 127, 128 to 255, ...) at most 6 rows name the same one
- gate_pre: bfloat16 [32, 1536, 4096], P('expert', None, 'etp'), may hold values from -6 to 6
- up_pre: bfloat16 [32, 1536, 4096], P('expert', None, 'etp'), may hold values from -6 to 6
- w_gate: bfloat16 [32, 2560, 4096], P('expert', None, 'etp'), may hold values from -0.125 to 0.125
- w_up: bfloat16 [32, 2560, 4096], P('expert', None, 'etp'), may hold values from -0.125 to 0.125
- w_down: bfloat16 [32, 4096, 2560], P('expert', 'etp'), may hold values from -0.09375 to 0.09375
Outputs:
- token_grad: bfloat16 [32768, 2560], P(('expert', 'etp'))
- router_grad: float32 [2560, 32], replicated
Inputs may be any that keep to these rules, and one draw needn't show every extreme that they name: `expert_choice`: within the 128 tokens of one device no expert is chosen more than 6 times, and in every draw some expert is chosen exactly 6 times by the tokens of some device.
All inputs are finite; a program needn't handle non-finite values.
Results may differ from a plain program's by a relative error of at most 0.015.
Values may be sent and summed in bfloat16 or wider, within the bound.
No kernel may reach another device: no remote copies, remote signals or barrier semaphores. Data moves between devices by JAX's collectives and lax.ppermute only.
A program may use at most 128 MiB of HBM per device.

v0:
```python
import jax
import jax.numpy as jnp
from jax import lax
from jax.sharding import PartitionSpec as P


def local(tokens, grad_out, router_weight, expert_choice, gate_pre, up_pre, w_gate, w_up, w_down):
    width = tokens.shape[1]
    experts = router_weight.shape[1]
    n_expert = lax.axis_size("expert")
    n_etp = lax.axis_size("etp")
    capacity = gate_pre.shape[1] // (n_expert * n_etp)
    contract = (((1,), (1,)), ((), ()))
    chosen_ids = expert_choice[:, 0]
    picked = chosen_ids[:, None] == jnp.arange(experts, dtype=jnp.int32)[None, :]
    logits = jnp.dot(tokens, router_weight, preferred_element_type=jnp.float32)
    score = jax.nn.sigmoid(jnp.sum(jnp.where(picked, logits, 0.0), axis=1))
    counts = picked.astype(jnp.int32)
    earlier = jnp.cumsum(counts, axis=0) - counts
    position = jnp.sum(earlier * counts, axis=1)
    target = chosen_ids * capacity + position
    placed = jnp.arange(experts * capacity, dtype=jnp.int32)[:, None] == target[None, :]
    onehot = placed.astype(jnp.bfloat16)
    outgoing = jnp.dot(onehot, grad_out, preferred_element_type=jnp.float32).astype(jnp.bfloat16)
    own = lax.all_to_all(outgoing, "expert", split_axis=0, concat_axis=0, tiled=True)
    arrived = lax.all_gather(own, "etp", axis=0, tiled=True)
    d_hidden = lax.dot_general(arrived, w_down[0], contract, preferred_element_type=jnp.float32)
    gate_f = gate_pre[0].astype(jnp.float32)
    up_f = up_pre[0].astype(jnp.float32)
    sig = jax.nn.sigmoid(gate_f)
    d_gate = (d_hidden * up_f * sig * (1.0 + gate_f * (1.0 - sig))).astype(jnp.bfloat16)
    d_up = (d_hidden * gate_f * sig).astype(jnp.bfloat16)
    terms = (
        lax.dot_general(d_gate, w_gate[0], contract, preferred_element_type=jnp.float32)
        + lax.dot_general(d_up, w_up[0], contract, preferred_element_type=jnp.float32)
    ).astype(jnp.bfloat16)
    summed = lax.psum_scatter(terms, "etp", scatter_dimension=0, tiled=True)
    returned = lax.all_to_all(summed, "expert", split_axis=0, concat_axis=0, tiled=True)
    fetched = lax.dot_general(
        onehot, returned, (((0,), (0,)), ((), ())), preferred_element_type=jnp.float32
    )
    inputs = tokens.astype(jnp.float32)
    d_logit = jnp.sum(inputs * fetched, axis=1) * score * (1.0 - score)
    column = lax.dot_general(
        picked.astype(jnp.bfloat16), router_weight, contract, preferred_element_type=jnp.float32
    )
    token_grad = (score[:, None] * fetched + d_logit[:, None] * column).astype(jnp.bfloat16)
    weighted = jnp.where(picked, d_logit[:, None], 0.0)
    local_terms = lax.dot_general(
        weighted,
        inputs,
        (((0,), (0,)), ((), ())),
        precision=lax.Precision.HIGHEST,
        preferred_element_type=jnp.float32,
    )
    mine = lax.all_to_all(
        local_terms.reshape(n_etp, experts // n_etp, width),
        "etp",
        split_axis=0,
        concat_axis=0,
        tiled=True,
    )
    mine = jnp.sum(mine, axis=0)
    mine = lax.psum(mine, "expert")
    router_grad = lax.all_gather(mine, "etp", axis=0, tiled=True).T
    return (token_grad, router_grad)


def solution(mesh):
    placed = (
        P(("expert", "etp"), None),
        P(("expert", "etp"), None),
        P(),
        P(("expert", "etp"), None),
        P("expert", None, "etp"),
        P("expert", None, "etp"),
        P("expert", None, "etp"),
        P("expert", None, "etp"),
        P("expert", "etp", None),
    )
    return jax.shard_map(
        local,
        mesh=mesh,
        in_specs=placed,
        out_specs=(P(("expert", "etp"), None), P()),
        check_vma=False,
    )
```

profile of v0, /device:TPU:1, one launch (start us, length us, event | category | flops | bytes accessed | tf_op | source)
XLA Modules:
  0.0 423.1 jit_solution(13606596880845416231)
XLA Ops:
  7.2 0.8 fusion.29
  9.7 2.5 convolution_convert_fusion
  12.2 2.3 all_to_all.19
  14.4 46.0 %all_to_all.29 = bf16[32,6,2560]{2,1,0:T(8,128)(2,1)} all-to-all(bf16[32,6,2560]{2,1,0:T(8,128)(2,1)} %all_to_all.19), channel_id=1, replica_groups=mesh['expert'=32,'etp'=8] {'expert'}, dimensions={0} | all-to-all | bytes 1966080 | tf_op jit(solution)/shard_map/all_to_all | solution.py:25
  60.4 2.3 all_to_all.21
  62.8 47.8 %all-gather.3.cloned.1.call-done = bf16[1536,2560]{1,0:T(8,128)(2,1)} async-done(((bf16[192,2560]{1,0:T(8,128)(2,1)}), bf16[1536,2560]{1,0:T(8,128)(2,1)}) %all-gather.3.cloned.1.call-update) | async-done | bytes 7864336 | tf_op jit(solution)/shard_map/all_gather | solution.py:26
  110.6 7.5 %fusion.14 = f32[1536,512]{1,0:T(8,128)S(1)} fusion(bf16[1536,2560]{1,0:T(8,128)(2,1)} %all-gather.3.cloned.1.call-done, bf16[1,512,2560]{2,1,0:T(8,128)(2,1)} %param.17), kind=kOutput, calls=%fused_computation.21 | convolution fusion | flops 4026531840 | bytes 13631488 | tf_op jit(solution)/shard_map/dot_general | solution.py:27
  118.1 1.7 copy-done.6
  119.8 9.8 %fusion.12 = f32[1536,2560]{1,0:T(8,128)} fusion(bf16[1,2560,512]{2,1,0:T(8,128)(2,1)S(1)} %copy-done, f32[1536,512]{1,0:T(8,128)S(1)} %fusion.14, bf16[1,1536,512]{2,1,0:T(8,128)(2,1)S(1)} %copy-done.4, bf16[1,1536,512]{2,1,0:T(8,128)(2,1)S(1)} %copy-done.5), kind=kOutput, calls=%fused_computation.19 | convolution fusion | flops 4035969024 | bytes 24641536 | tf_op jit(solution)/shard_map/dot_general | solution.py:34
  129.6 15.2 %add_convert_fusion = bf16[1536,2560]{1,0:T(8,128)(2,1)} fusion(f32[1536,2560]{1,0:T(8,128)} %fusion.12, bf16[1,2560,512]{2,1,0:T(8,128)(2,1)} %param.16, f32[1536,512]{1,0:T(8,128)} %copy-done.6, bf16[1,1536,512]{2,1,0:T(8,128)(2,1)} %param.13), kind=kOutput, calls=%fused_computation | convolution fusion | flops 4039901184 | bytes 30932992 | tf_op jit(solution)/shard_map/dot_general | solution.py:35
  144.9 51.8 %reduce-scatter.2.cloned.1.call-done = bf16[192,2560]{1,0:T(8,128)(2,1)} async-done(((bf16[1536,2560]{1,0:T(8,128)(2,1)}), bf16[192,2560]{1,0:T(8,128)(2,1)}) %reduce-scatter.2.cloned.1.call-update) | async-done | bytes 983056 | tf_op jit(solution)/shard_map/reduce_scatter | solution.py:37
  196.8 2.3 all_to_all.22
  199.0 9.7 %all-to-all-start.1 = ((bf16[32,6,2560]{2,1,0:T(8,128)(2,1)}), bf16[32,6,2560]{2,1,0:T(8,128)(2,1)}, u32[]{:S(2)}, u32[]{:S(2)}) async-start(bf16[32,6,2560]{2,1,0:T(8,128)(2,1)} %all_to_all.22), calls=%async_computation.2 | async-start | bytes 2621440 | tf_op jit(solution)/shard_map/all_to_all | solution.py:38
  209.1 30.4 %all-to-all-done.1 = bf16[32,6,2560]{2,1,0:T(8,128)(2,1)} async-done(((bf16[32,6,2560]{2,1,0:T(8,128)(2,1)}), bf16[32,6,2560]{2,1,0:T(8,128)(2,1)}, u32[]{:S(2)}, u32[]{:S(2)}) %all-to-all-start.1) | async-done | bytes 983072 | tf_op jit(solution)/shard_map/all_to_all | solution.py:38
  239.5 2.2 all_to_all.24
  241.7 2.7 multiply_reduce_fusion
  244.4 1.1 fusion.27
  245.5 1.8 reshape.36
  247.3 7.3 %all-to-all-start.2 = ((f32[8,4,2560]{2,1,0:T(4,128)}), f32[8,4,2560]{2,1,0:T(4,128)S(1)}, u32[]{:S(2)}, u32[]{:S(2)}) async-start(f32[8,4,2560]{2,1,0:T(4,128)} %reshape.36), calls=%async_computation.3 | async-start | bytes 655360 | tf_op jit(solution)/shard_map/all_to_all | solution.py:56
  254.6 2.5 fusion.1
  257.1 4.6 %all-to-all-done.2 = f32[8,4,2560]{2,1,0:T(4,128)S(1)} async-done(((f32[8,4,2560]{2,1,0:T(4,128)}), f32[8,4,2560]{2,1,0:T(4,128)S(1)}, u32[]{:S(2)}, u32[]{:S(2)}) %all-to-all-start.2) | async-done | bytes 327712 | tf_op jit(solution)/shard_map/all_to_all | solution.py:56
  261.8 112.4 %psum.7 = f32[4,2560]{1,0:T(4,128)S(1)} all-reduce(f32[4,2560]{1,0:T(4,128)S(1)} %reduce_sum.39), channel_id=1, replica_groups=mesh['expert'=32,'etp'=8] {'expert'}, use_global_device_ids=true, to_apply=%region_6.7 | all-reduce | flops 10240 | bytes 81920 | tf_op jit(solution)/shard_map/psum | solution.py:64
  374.2 41.3 %all-gather = f32[8,4,2560]{2,1,0:T(4,128)S(1)} all-gather(f32[1,4,2560]{2,1,0:T(4,128)S(1)} %bitcast.37), channel_id=1, replica_groups=mesh['expert'=32,'etp'=8] {'etp'}, dimensions={0}, use_global_device_ids=true | all-gather | bytes 368640 | tf_op jit(solution)/shard_map/all_gather | solution.py:65
  415.5 0.8 reshape.40
  (25 shorter events, 2.2 us)
Async XLA Ops:
  7.2 112.6 %copy-start = (bf16[1,2560,512]{2,1,0:T(8,128)(2,1)S(1)}, bf16[1,2560,512]{2,1,0:T(8,128)(2,1)}, u32[]{:S(2)}) copy-start(bf16[1,2560,512]{2,1,0:T(8,128)(2,1)} %param.15) | copy-start | bytes 7864324
  7.2 103.4 %all-gather.3.cloned.1.call-start = ((), (), s32[]{:S(2)}) async-start(), calls=%async_computation.4 | async-start | bytes 8847360 | tf_op jit(solution)/shard_map/all_gather | solution.py:26
  62.7 134.0 %reduce-scatter.2.cloned.1.call-start = ((), (), s32[]{:S(2)}) async-start(), calls=%async_computation.5 | async-start | bytes 8847360 | tf_op jit(solution)/shard_map/reduce_scatter | solution.py:37
  110.6 9.3 %copy-start.4 = (bf16[1,1536,512]{2,1,0:T(8,128)(2,1)S(1)}, bf16[1,1536,512]{2,1,0:T(8,128)(2,1)}, u32[]{:S(2)}) copy-start(bf16[1,1536,512]{2,1,0:T(8,128)(2,1)} %param.14) | copy-start | bytes 4718596
  110.6 9.3 %copy-start.5 = (bf16[1,1536,512]{2,1,0:T(8,128)(2,1)S(1)}, bf16[1,1536,512]{2,1,0:T(8,128)(2,1)}, u32[]{:S(2)}) copy-start(bf16[1,1536,512]{2,1,0:T(8,128)(2,1)} %param.13) | copy-start | bytes 4718596
  118.1 1.7 copy-start.6
  144.9 63.8 %copy-start.1 = (bf16[128,2560]{1,0:T(8,128)(2,1)S(1)}, bf16[128,2560]{1,0:T(8,128)(2,1)}, u32[]{:S(2)}) copy-start(bf16[128,2560]{1,0:T(8,128)(2,1)} %param.9) | copy-start | bytes 1966084
  144.9 63.8 %copy-start.2 = (bf16[2560,32]{0,1:T(8,128)(2,1)S(1)}, bf16[2560,32]{0,1:T(8,128)(2,1)}, u32[]{:S(2)}) copy-start(bf16[2560,32]{0,1:T(8,128)(2,1)} %param.11) | copy-start | bytes 491524
  144.9 63.8 %copy-start.3 = (s32[128,1]{0,1:T(1,128)S(1)}, s32[128,1]{0,1:T(1,128)}, u32[]{:S(2)}) copy-start(s32[128,1]{0,1:T(1,128)} %param.12) | copy-start | bytes 1540
  199.0 40.4 %all-to-all-start.1 = ((bf16[32,6,2560]{2,1,0:T(8,128)(2,1)}), bf16[32,6,2560]{2,1,0:T(8,128)(2,1)}, u32[]{:S(2)}, u32[]{:S(2)}) async-start(bf16[32,6,2560]{2,1,0:T(8,128)(2,1)} %all_to_all.22), calls=%async_computation.2 | async-start | bytes 2621440 | tf_op jit(solution)/shard_map/all_to_all | solution.py:38
  247.3 14.4 %all-to-all-start.2 = ((f32[8,4,2560]{2,1,0:T(4,128)}), f32[8,4,2560]{2,1,0:T(4,128)S(1)}, u32[]{:S(2)}, u32[]{:S(2)}) async-start(f32[8,4,2560]{2,1,0:T(4,128)} %reshape.36), calls=%async_computation.3 | async-start | bytes 655360 | tf_op jit(solution)/shard_map/all_to_all | solution.py:56
Sparse Core Ops, SparseCore 0:
  62.9 47.6 all-gather.2
  145.0 51.6 reduce-scatter.1
where the time goes:
time: 424 us; the launch traced here: 423 us
  blocking collectives  200 us (47%)
  waiting for transfers between devices  135 us (32%)
  matrix products  41.7 us (10%)
  starting transfers between devices  17.1 us (4%)
  between operations  14.1 us (3%)
  local copies, waits for them, and re-layouts  13.6 us (3%)
    psum x1, blocking collectives, local(): mine = lax.psum(mine, 'expert')  112 us
    reduce_scatter x1, waiting for transfers between devices, local(): summed = lax.psum_scatter(terms, 'etp', scatter_dimension=0, tiled=True)  51.8 us
    all_gather x1, waiting for transfers between devices, local(): arrived = lax.all_gather(own, 'etp', axis=0, tiled=True)  47.8 us
    all_to_all x1, blocking collectives, local(): lax.all_to_all(outgoing, 'expert', split_axis=0, concat_axis=0, tiled=True)  46 us
    all_gather x1, blocking collectives, local(): router_grad = lax.all_gather(mine, 'etp', axis=0, tiled=True).T  41.3 us
    all_to_all x1, waiting for transfers between devices, local(): lax.all_to_all(summed, 'expert', split_axis=0, concat_axis=0, tiled=True)  30.4 us
    dot_general x1, matrix products, local(): lax.dot_general(d_up, w_up[0], contract, preferred_element_type=jnp.float32)  15.2 us
    dot_general x1, matrix products, local(): lax.dot_general(d_gate, w_gate[0], contract, preferred_element_type=jnp.f...  9.81 us
  transfers between devices with their start and end apart: 4, of which 4 were waited for; matrix products, arithmetic and copies ran while one was open for 1% of the time, Pallas kernels for 0%

commit v1 on v0

--- a/solution.py
+++ b/solution.py
@@ -2,6 +2,27 @@
 import jax.numpy as jnp
 from jax import lax
 from jax.sharding import PartitionSpec as P
+
+
+def collect(x, axis, dim):
+    devices, here, rows = (lax.axis_size(axis), lax.axis_index(axis), x.shape[dim])
+    right = [(i, (i + 1) % devices) for i in range(devices)]
+    behind = [(i, (i - 1) % devices) for i in range(devices)]
+    result = jnp.zeros((*x.shape[:dim], devices * rows, *x.shape[dim + 1 :]), x.dtype)
+    result = lax.dynamic_update_slice_in_dim(result, x, here * rows, axis=dim)
+    from_left = from_right = x
+    half = devices // 2
+    for step in range(1, half + 1):
+        from_left = lax.ppermute(from_left, axis, right)
+        result = lax.dynamic_update_slice_in_dim(
+            result, from_left, (here - step) % devices * rows, axis=dim
+        )
+        if step < devices - half:
+            from_right = lax.ppermute(from_right, axis, behind)
+            result = lax.dynamic_update_slice_in_dim(
+                result, from_right, (here + step) % devices * rows, axis=dim
+            )
+    return result
 
 
 def local(tokens, grad_out, router_weight, expert_choice, gate_pre, up_pre, w_gate, w_up, w_down):
@@ -62,7 +83,7 @@
     )
     mine = jnp.sum(mine, axis=0)
     mine = lax.psum(mine, "expert")
-    router_grad = lax.all_gather(mine, "etp", axis=0, tiled=True).T
+    router_grad = collect(mine, "etp", 0).T
     return (token_grad, router_grad)
 
 

time: 424 us -> 426 us (level)
  blocking collectives: 200 us -> 158 us
  starting transfers between devices: 17.1 us -> 52.9 us
  waiting for transfers between devices: 135 us -> 142 us
    all_gather x1 -> x0, blocking collectives: 41.3 us -> none  [local(): router_grad = lax.all_gather(mine, 'etp', axis=0, tiled=True).T]
    ppermute x0 -> x7, starting transfers between devices: none -> 35.8 us  [the longest x4 33.1 us: collect(): from_left = lax.ppermute(from_left, axis, right)]
    ppermute x0 -> x7, waiting for transfers between devices: none -> 7.09 us  [the longest x4 6.23 us: collect(): from_left = lax.ppermute(from_left, axis, right)]
  transfers between devices with their start and end apart: 4 -> 11, of which waited for: 4 -> 11; matrix products, arithmetic and copies ran while one was open for 1% -> 1% of each run, Pallas kernels for 0% -> 0%
where the time goes in v1:
time: 426 us; the launch traced here: 424 us
  blocking collectives  158 us (37%)
  waiting for transfers between devices  142 us (33%)
  starting transfers between devices  52.9 us (12%)
  matrix products  41.5 us (10%)
  between operations  14.2 us (3%)
  local copies, waits for them, and re-layouts  13.7 us (3%)
    psum x1, blocking collectives, local(): mine = lax.psum(mine, 'expert')  112 us
    reduce_scatter x1, waiting for transfers between devices, local(): summed = lax.psum_scatter(terms, 'etp', scatter_dimension=0, tiled=True)  51.8 us
    all_gather x1, waiting for transfers between devices, local(): arrived = lax.all_gather(own, 'etp', axis=0, tiled=True)  47.8 us
    all_to_all x1, blocking collectives, local(): lax.all_to_all(outgoing, 'expert', split_axis=0, concat_axis=0, tiled=True)  46 us
    ppermute x4, starting transfers between devices, collect(): from_left = lax.ppermute(from_left, axis, right)  33.1 us
    all_to_all x1, waiting for transfers between devices, local(): lax.all_to_all(summed, 'expert', split_axis=0, concat_axis=0, tiled=True)  30.4 us
    dot_general x1, matrix products, local(): lax.dot_general(d_up, w_up[0], contract, preferred_element_type=jnp.float32)  15.2 us
    all_to_all x1, starting transfers between devices, local(): lax.all_to_all(summed, 'expert', split_axis=0, concat_axis=0, tiled=True)  9.68 us
  transfers between devices with their start and end apart: 11, of which 11 were waited for; matrix products, arithmetic and copies ran while one was open for 1% of the time, Pallas kernels for 0%

profile of v1, /device:TPU:1, one launch (start us, length us, event | category | flops | bytes accessed | tf_op | source)
XLA Modules:
  0.0 424.3 jit_solution(1007545511862666476)
XLA Ops:
  9.7 2.4 convolution_convert_fusion
  12.2 2.3 all_to_all.19
  14.4 46.0 %all_to_all.29 = bf16[32,6,2560]{2,1,0:T(8,128)(2,1)} all-to-all(bf16[32,6,2560]{2,1,0:T(8,128)(2,1)} %all_to_all.19), channel_id=1, replica_groups=mesh['expert'=32,'etp'=8] {'expert'}, dimensions={0} | all-to-all | bytes 1966080 | tf_op jit(solution)/shard_map/all_to_all | solution.py:46
  60.4 2.3 all_to_all.21
  62.8 47.8 %all-gather.2.cloned.1.call-done = bf16[1536,2560]{1,0:T(8,128)(2,1)} async-done(((bf16[192,2560]{1,0:T(8,128)(2,1)}), bf16[1536,2560]{1,0:T(8,128)(2,1)}) %all-gather.2.cloned.1.call-update) | async-done | bytes 7864336 | tf_op jit(solution)/shard_map/all_gather | solution.py:47
  110.6 7.5 %fusion.14 = f32[1536,512]{1,0:T(8,128)S(1)} fusion(bf16[1536,2560]{1,0:T(8,128)(2,1)} %all-gather.2.cloned.1.call-done, bf16[1,512,2560]{2,1,0:T(8,128)(2,1)} %param.17), kind=kOutput, calls=%fused_computation.21 | convolution fusion | flops 4026531840 | bytes 13631488 | tf_op jit(solution)/shard_map/dot_general | solution.py:48
  118.1 1.7 copy-done.7
  119.8 9.6 %fusion.12 = f32[1536,2560]{1,0:T(8,128)} fusion(bf16[1,2560,512]{2,1,0:T(8,128)(2,1)S(1)} %copy-done, f32[1536,512]{1,0:T(8,128)S(1)} %fusion.14, bf16[1,1536,512]{2,1,0:T(8,128)(2,1)S(1)} %copy-done.5, bf16[1,1536,512]{2,1,0:T(8,128)(2,1)S(1)} %copy-done.6), kind=kOutput, calls=%fused_computation.19 | convolution fusion | flops 4035969024 | bytes 24641536 | tf_op jit(solution)/shard_map/dot_general | solution.py:55
  129.4 15.2 %add_convert_fusion = bf16[1536,2560]{1,0:T(8,128)(2,1)} fusion(f32[1536,2560]{1,0:T(8,128)} %fusion.12, bf16[1,2560,512]{2,1,0:T(8,128)(2,1)} %param.16, f32[1536,512]{1,0:T(8,128)} %copy-done.7, bf16[1,1536,512]{2,1,0:T(8,128)(2,1)} %param.13), kind=kOutput, calls=%fused_computation | convolution fusion | flops 4039901184 | bytes 30932992 | tf_op jit(solution)/shard_map/dot_general | solution.py:56
  144.7 51.8 %reduce-scatter.2.cloned.1.call-done = bf16[192,2560]{1,0:T(8,128)(2,1)} async-done(((bf16[1536,2560]{1,0:T(8,128)(2,1)}), bf16[192,2560]{1,0:T(8,128)(2,1)}) %reduce-scatter.2.cloned.1.call-update) | async-done | bytes 983056 | tf_op jit(solution)/shard_map/reduce_scatter | solution.py:58
  196.6 2.3 all_to_all.22
  198.8 9.7 %all-to-all-start.1 = ((bf16[32,6,2560]{2,1,0:T(8,128)(2,1)}), bf16[32,6,2560]{2,1,0:T(8,128)(2,1)}, u32[]{:S(2)}, u32[]{:S(2)}) async-start(bf16[32,6,2560]{2,1,0:T(8,128)(2,1)} %all_to_all.22), calls=%async_computation.2 | async-start | bytes 2621440 | tf_op jit(solution)/shard_map/all_to_all | solution.py:59
  208.9 30.4 %all-to-all-done.1 = bf16[32,6,2560]{2,1,0:T(8,128)(2,1)} async-done(((bf16[32,6,2560]{2,1,0:T(8,128)(2,1)}), bf16[32,6,2560]{2,1,0:T(8,128)(2,1)}, u32[]{:S(2)}, u32[]{:S(2)}) %all-to-all-start.1) | async-done | bytes 983072 | tf_op jit(solution)/shard_map/all_to_all | solution.py:59
  239.2 2.3 all_to_all.24
  241.5 2.7 multiply_reduce_fusion
  245.3 1.8 reshape.36
  247.1 7.3 %all-to-all-start.2 = ((f32[8,4,2560]{2,1,0:T(4,128)}), f32[8,4,2560]{2,1,0:T(4,128)S(1)}, u32[]{:S(2)}, u32[]{:S(2)}) async-start(f32[8,4,2560]{2,1,0:T(4,128)} %reshape.36), calls=%async_computation.3 | async-start | bytes 655360 | tf_op jit(solution)/shard_map/all_to_all | solution.py:77
  254.4 2.5 fusion.1
  256.9 4.6 %all-to-all-done.2 = f32[8,4,2560]{2,1,0:T(4,128)S(1)} async-done(((f32[8,4,2560]{2,1,0:T(4,128)}), f32[8,4,2560]{2,1,0:T(4,128)S(1)}, u32[]{:S(2)}, u32[]{:S(2)}) %all-to-all-start.2) | async-done | bytes 327712 | tf_op jit(solution)/shard_map/all_to_all | solution.py:77
  261.6 112.1 %psum.7 = f32[4,2560]{1,0:T(4,128)S(1)} all-reduce(f32[4,2560]{1,0:T(4,128)S(1)} %reduce_sum.39), channel_id=1, replica_groups=mesh['expert'=32,'etp'=8] {'expert'}, use_global_device_ids=true, to_apply=%region_6.7 | all-reduce | flops 10240 | bytes 81920 | tf_op jit(solution)/shard_map/psum | solution.py:85
  373.7 28.6 %collective-permute-start = (f32[4,2560]{1,0:T(4,128)S(1)}, f32[4,2560]{1,0:T(4,128)S(1)}, u32[]{:S(2)}, u32[]{:S(2)}) collective-permute-start(f32[4,2560]{1,0:T(4,128)S(1)} %psum.7), channel_id=1, source_target_pairs={{0,1},{1,2},{2,3},{3,4},{4,5},{5,6},{6,7},{7,0},{8,9},{9,10},{10,1... | collective-permute-start | bytes 122888 | tf_op jit(solution)/shard_map/ppermute | solution.py:16
  403.4 2.3 collective-permute-start.2
  409.4 2.0 collective-permute-start.5
  412.9 3.9 collective-permute-done.6
  (48 shorter events, 11.2 us)
Async XLA Ops:
  7.2 112.6 %copy-start = (bf16[1,2560,512]{2,1,0:T(8,128)(2,1)S(1)}, bf16[1,2560,512]{2,1,0:T(8,128)(2,1)}, u32[]{:S(2)}) copy-start(bf16[1,2560,512]{2,1,0:T(8,128)(2,1)} %param.15) | copy-start | bytes 7864324
  7.2 103.4 %all-gather.2.cloned.1.call-start = ((), (), s32[]{:S(2)}) async-start(), calls=%async_computation.4 | async-start | bytes 8847360 | tf_op jit(solution)/shard_map/all_gather | solution.py:47
  62.7 133.8 %reduce-scatter.2.cloned.1.call-start = ((), (), s32[]{:S(2)}) async-start(), calls=%async_computation.5 | async-start | bytes 8847360 | tf_op jit(solution)/shard_map/reduce_scatter | solution.py:58
  110.5 9.3 %copy-start.5 = (bf16[1,1536,512]{2,1,0:T(8,128)(2,1)S(1)}, bf16[1,1536,512]{2,1,0:T(8,128)(2,1)}, u32[]{:S(2)}) copy-start(bf16[1,1536,512]{2,1,0:T(8,128)(2,1)} %param.14) | copy-start | bytes 4718596
  110.5 9.3 %copy-start.6 = (bf16[1,1536,512]{2,1,0:T(8,128)(2,1)S(1)}, bf16[1,1536,512]{2,1,0:T(8,128)(2,1)}, u32[]{:S(2)}) copy-start(bf16[1,1536,512]{2,1,0:T(8,128)(2,1)} %param.13) | copy-start | bytes 4718596
  118.1 1.7 copy-start.7
  144.7 63.8 %copy-start.1 = (bf16[128,2560]{1,0:T(8,128)(2,1)S(1)}, bf16[128,2560]{1,0:T(8,128)(2,1)}, u32[]{:S(2)}) copy-start(bf16[128,2560]{1,0:T(8,128)(2,1)} %param.9) | copy-start | bytes 1966084
  144.7 63.8 %copy-start.2 = (bf16[2560,32]{0,1:T(8,128)(2,1)S(1)}, bf16[2560,32]{0,1:T(8,128)(2,1)}, u32[]{:S(2)}) copy-start(bf16[2560,32]{0,1:T(8,128)(2,1)} %param.11) | copy-start | bytes 491524
  144.7 63.8 %copy-start.4 = (s32[128,1]{0,1:T(1,128)S(1)}, s32[128,1]{0,1:T(1,128)}, u32[]{:S(2)}) copy-start(s32[128,1]{0,1:T(1,128)} %param.12) | copy-start | bytes 1540
  198.8 40.4 %all-to-all-start.1 = ((bf16[32,6,2560]{2,1,0:T(8,128)(2,1)}), bf16[32,6,2560]{2,1,0:T(8,128)(2,1)}, u32[]{:S(2)}, u32[]{:S(2)}) async-start(bf16[32,6,2560]{2,1,0:T(8,128)(2,1)} %all_to_all.22), calls=%async_computation.2 | async-start | bytes 2621440 | tf_op jit(solution)/shard_map/all_to_all | solution.py:59
  247.1 14.4 %all-to-all-start.2 = ((f32[8,4,2560]{2,1,0:T(4,128)}), f32[8,4,2560]{2,1,0:T(4,128)S(1)}, u32[]{:S(2)}, u32[]{:S(2)}) async-start(f32[8,4,2560]{2,1,0:T(4,128)} %reshape.36), calls=%async_computation.3 | async-start | bytes 655360 | tf_op jit(solution)/shard_map/all_to_all | solution.py:77
  373.7 29.7 %collective-permute-start = (f32[4,2560]{1,0:T(4,128)S(1)}, f32[4,2560]{1,0:T(4,128)S(1)}, u32[]{:S(2)}, u32[]{:S(2)}) collective-permute-start(f32[4,2560]{1,0:T(4,128)S(1)} %psum.7), channel_id=1, source_target_pairs={{0,1},{1,2},{2,3},{3,4},{4,5},{5,6},{6,7},{7,0},{8,9},{9,10},{10,1... | collective-permute-start | bytes 122888 | tf_op jit(solution)/shard_map/ppermute | solution.py:16
  402.3 3.7 collective-permute-start.1
  403.4 4.1 collective-permute-start.2
  406.0 3.4 collective-permute-start.3
  407.5 4.6 %collective-permute-start.4 = (f32[4,2560]{1,0:T(4,128)S(1)}, f32[4,2560]{1,0:T(4,128)S(1)}, u32[]{:S(2)}, u32[]{:S(2)}) collective-permute-start(f32[4,2560]{1,0:T(4,128)S(1)} %collective-permute-done.2), channel_id=1, source_target_pairs={{0,1},{1,2},{2,3},{3,4},{4,5},{5,6},{6,7},{7,0},{8,9},{9,10},{10,1... | collective-permute-start | bytes 122888 | tf_op jit(solution)/shard_map/ppermute | solution.py:16
  409.4 3.4 collective-permute-start.5
  412.1 4.6 %collective-permute-start.6 = (f32[4,2560]{1,0:T(4,128)S(1)}, f32[4,2560]{1,0:T(4,128)S(1)}, u32[]{:S(2)}, u32[]{:S(2)}) collective-permute-start(f32[4,2560]{1,0:T(4,128)S(1)} %collective-permute-done.4), channel_id=1, source_target_pairs={{0,1},{1,2},{2,3},{3,4},{4,5},{5,6},{6,7},{7,0},{8,9},{9,10},{10,1... | collective-permute-start | bytes 122888 | tf_op jit(solution)/shard_map/ppermute | solution.py:16
  416.7 0.7 copy-start.3
Sparse Core Ops, SparseCore 0:
  62.8 47.6 all-gather.1
  144.8 51.6 reduce-scatter.1
